TPU v7x, 512 devices: a whole 4x4x16 slice. The times are simulated.
512 devices in a mesh: freq: 32 (over z_lo, x), src: 2 (over z_hi), rcv: 8 (over y, core).
Axes of the slice: x: 4, y: 4, z: 16 (z_hi: 2, z_lo: 8; z = z_hi * 8 + z_lo), core: 2. Of those that a mesh axis runs over, the one named last changes fastest.
Arguments:
- traces: float32 [1024, 1024, 256], P(('src', 'freq'), 'rcv'), may hold values from -6 to 6
Outputs:
- multiples: float32 [2, 96, 1024, 1024], P(None, 'freq', 'src', 'rcv')
All inputs are finite; a program needn't handle non-finite values.
Results may differ from a plain program's by a relative error of at most 0.000098.
Values sent between devices are 32-bit elements; how exact they have to be, the bound alone decides.
A program may use at most 64 MiB of HBM per device.

v0:
```python
import math
import jax
import jax.numpy as jnp
from jax import lax
from jax.sharding import PartitionSpec as P

N = 1024
FPD = 3


def dft_matrix(n_time, n_freq):
    times = jnp.arange(n_time, dtype=jnp.int32)
    bins = jnp.arange(n_freq, dtype=jnp.int32)
    phase = times[:, None] * bins[None, :] % n_time
    angle = phase.astype(jnp.float32) * (2.0 * math.pi / n_time)
    both = jnp.stack([jnp.cos(angle), -jnp.sin(angle)], axis=-1)
    return both.reshape(n_time, 2 * n_freq) * (1.0 / math.sqrt(n_time))


def batched_dot(left, right):
    return jnp.einsum(
        "mgq,mqn->mgn",
        left,
        right,
        precision=lax.Precision.HIGHEST,
        preferred_element_type=jnp.float32,
    )


def complex_product(left_re, left_im, right_re, right_im):
    real_part = batched_dot(left_re, right_re) - batched_dot(left_im, right_im)
    imag_part = batched_dot(left_re, right_im) + batched_dot(left_im, right_re)
    return (real_part, imag_part)


def per_device(traces):
    n_time = traces.shape[2]
    n_freq = FPD * lax.axis_size("freq")
    dft_table = dft_matrix(n_time, n_freq)
    spectra = jnp.einsum(
        "srt,tk->ksr",
        traces,
        dft_table,
        precision=lax.Precision.HIGHEST,
        preferred_element_type=jnp.float32,
    )
    regrouped = lax.all_to_all(spectra, "freq", split_axis=0, concat_axis=1, tiled=True)
    src_rows = regrouped.shape[1]
    rcv_cols = regrouped.shape[2]
    split_parts = regrouped.reshape(FPD, 2, src_rows, rcv_cols)
    local_re = split_parts[:, 0]
    local_im = split_parts[:, 1]
    col_re, col_im = (
        lax.all_gather(local_re, "src", axis=1, tiled=True),
        lax.all_gather(local_im, "src", axis=1, tiled=True),
    )
    piece_re = lax.all_gather(local_re, "rcv", axis=2, tiled=True)
    piece_im = lax.all_gather(local_im, "rcv", axis=2, tiled=True)
    real_part, imag_part = complex_product(piece_re, piece_im, col_re, col_im)
    scale = -1.0 / math.sqrt(N)
    return jnp.stack([real_part, imag_part]) * scale


def solution(mesh):
    in_specs = (P(("src", "freq"), "rcv", None),)
    out_specs = P(None, "freq", "src", "rcv")
    return jax.shard_map(
        per_device, mesh=mesh, in_specs=in_specs, out_specs=out_specs, check_vma=False
    )
```

profile of v0, /device:TPU:1, one launch (start us, length us, event | category | flops | bytes accessed | tf_op | source)
XLA Modules:
  0.0 411.7 jit_solution(3908307167513742405)
XLA Ops:
  6.5 0.4 sine_negate_fusion
  7.0 0.2 copy.14
  7.1 0.1 reshape.83
  7.3 0.8 copy-done
  8.1 2.3 fusion.39
  10.4 0.9 copy.15
  11.3 89.4 %all_to_all.15 = f32[192,16,128]{2,1,0:T(8,128)S(1)} all-to-all(f32[192,16,128]{2,1,0:T(8,128)S(1)} %copy.15), channel_id=1, replica_groups=mesh['freq'=32,'src'=2,'rcv'=8] {'freq'}, dimensions={0} | all-to-all | bytes 3145728 | tf_op jit(solution)/shard_map/all_to_all | solution.py:47
  100.7 0.1 copy.16
  100.9 1.3 slice_bitcast_fusion.1
  102.1 0.0 all-gather.13.cloned.1.call-start
  102.2 0.7 all-gather.13.cloned.1.call-update
  102.9 0.0 all-gather.15.cloned.1.call-start
  102.9 0.7 all-gather.15.cloned.1.call-update
  103.6 0.2 all-gather.9.cloned.1.call-start
  103.9 0.3 all-gather.9.cloned.1.call-update
  104.2 90.4 %all-gather.11.cloned.1.call-done = f32[3,1,1024,128]{3,2,0,1:T(8,128)} async-done(((f32[3,1,512,128]{3,2,0,1:T(8,128)}), f32[3,1,1024,128]{3,2,0,1:T(8,128)}) %all-gather.11.cloned.1.call-update) | async-done | bytes 1572880 | tf_op jit(solution)/shard_map/all_gather | solution.py:54
  194.6 48.8 %all-gather.13.cloned.1.call-done = f32[3,1,512,1024]{3,2,0,1:T(8,128)} async-done(((f32[3,1,512,128]{3,2,0,1:T(8,128)}), f32[3,1,512,1024]{3,2,0,1:T(8,128)}) %all-gather.13.cloned.1.call-update) | async-done | bytes 6291472 | tf_op jit(solution)/shard_map/all_gather | solution.py:58
  243.4 7.9 %fusion = f32[3,512,128]{2,1,0:T(8,128)S(1)} fusion(f32[3,1,512,1024]{3,2,0,1:T(8,128)} %all-gather.13.cloned.1.call-done, f32[3,1,1024,128]{3,2,0,1:T(8,128)} %all-gather.11.cloned.1.call-done), kind=kOutput, calls=%fused_computation | convolution fusion | flops 2415919104 | bytes 8650752 | tf_op jit(solution)/shard_map/mgq,mqn->mgn/dot_general | solution.py:21
  251.3 90.1 %all-gather.15.cloned.1.call-done = f32[3,1,1024,128]{3,2,0,1:T(8,128)} async-done(((f32[3,1,512,128]{3,2,0,1:T(8,128)}), f32[3,1,1024,128]{3,2,0,1:T(8,128)}) %all-gather.15.cloned.1.call-update) | async-done | bytes 1572880 | tf_op jit(solution)/shard_map/all_gather | solution.py:55
  341.4 8.8 %fusion.2 = f32[3,512,128]{2,1,0:T(8,128)} fusion(f32[3,1,512,1024]{3,2,0,1:T(8,128)} %all-gather.13.cloned.1.call-done, f32[3,1,1024,128]{3,2,0,1:T(8,128)} %all-gather.15.cloned.1.call-done), kind=kOutput, calls=%fused_computation.2 | convolution fusion | flops 2415919104 | bytes 8650752 | tf_op jit(solution)/shard_map/mgq,mqn->mgn/dot_general | solution.py:21
  350.2 39.8 %all-gather.9.cloned.1.call-done = f32[3,1,512,1024]{3,2,0,1:T(8,128)} async-done(((f32[3,1,512,128]{3,2,0,1:T(8,128)}), f32[3,1,512,1024]{3,2,0,1:T(8,128)}) %all-gather.9.cloned.1.call-update) | async-done | bytes 6291472 | tf_op jit(solution)/shard_map/all_gather | solution.py:57
  390.1 8.4 %fusion.22 = f32[1,3,512,128]{3,2,1,0:T(8,128)S(1)} fusion(f32[3,512,128]{2,1,0:T(8,128)S(1)} %fusion, f32[3,1,1024,128]{3,2,0,1:T(8,128)} %all-gather.15.cloned.1.call-done, f32[3,1,512,1024]{3,2,0,1:T(8,128)} %all-gather.9.cloned.1.call-done), kind=kOutput, calls=%fused_computation.15 | convolution fusion | flops 2416115712 | bytes 9437184 | tf_op jit(solution)/shard_map/mgq,mqn->mgn/dot_general | solution.py:21
  398.5 5.4 %fusion.27 = f32[1,3,512,128]{3,2,1,0:T(8,128)S(1)} fusion(f32[3,512,128]{2,1,0:T(8,128)S(1)} %copy-done.3, f32[3,1,1024,128]{3,2,0,1:T(8,128)S(1)} %copy-done.2, f32[3,1,512,1024]{3,2,0,1:T(8,128)S(1)} %copy-done.1), kind=kOutput, calls=%fused_computation.16 | convolution fusion | flops 2416115712 | bytes 9437184 | tf_op jit(solution)/shard_map/mgq,mqn->mgn/dot_general | solution.py:21
  403.9 1.2 maximum_multiply_fusion
  (10 shorter events, 0.0 us)
Async XLA Ops:
  6.5 1.6 copy-start
  6.5 188.0 %all-gather.11.cloned.1.call-start = ((), (), s32[]{:S(2)}) async-start(), calls=%async_computation.2 | async-start | bytes 2359296 | tf_op jit(solution)/shard_map/all_gather | solution.py:54
  102.1 141.2 %all-gather.13.cloned.1.call-start = ((), (), s32[]{:S(2)}) async-start(), calls=%async_computation.3 | async-start | bytes 7077888 | tf_op jit(solution)/shard_map/all_gather | solution.py:58
  102.9 238.5 %all-gather.15.cloned.1.call-start = ((), (), s32[]{:S(2)}) async-start(), calls=%async_computation.4 | async-start | bytes 2359296 | tf_op jit(solution)/shard_map/all_gather | solution.py:55
  103.6 286.5 %all-gather.9.cloned.1.call-start = ((), (), s32[]{:S(2)}) async-start(), calls=%async_computation.1 | async-start | bytes 7077888 | tf_op jit(solution)/shard_map/all_gather | solution.py:57
  390.1 8.4 %copy-start.1 = (f32[3,1,512,1024]{3,2,0,1:T(8,128)S(1)}, f32[3,1,512,1024]{3,2,0,1:T(8,128)}, u32[]{:S(2)}) copy-start(f32[3,1,512,1024]{3,2,0,1:T(8,128)} %all-gather.9.cloned.1.call-done) | copy-start | bytes 18874372
  390.1 8.4 %copy-start.2 = (f32[3,1,1024,128]{3,2,0,1:T(8,128)S(1)}, f32[3,1,1024,128]{3,2,0,1:T(8,128)}, u32[]{:S(2)}) copy-start(f32[3,1,1024,128]{3,2,0,1:T(8,128)} %all-gather.11.cloned.1.call-done) | copy-start | bytes 4718596
  390.1 8.4 %copy-start.3 = (f32[3,512,128]{2,1,0:T(8,128)S(1)}, f32[3,512,128]{2,1,0:T(8,128)}, u32[]{:S(2)}) copy-start(f32[3,512,128]{2,1,0:T(8,128)} %fusion.2) | copy-start | bytes 2359300
Sparse Core Ops, SparseCore 0:
  102.3 92.2 all-gather.10
  196.7 46.6 all-gather.12
  245.5 95.8 all-gather.14
  343.4 46.6 all-gather.8
where the time goes:
time: 412 us
  waiting for transfers between devices  271 us (66%)
  blocking collectives  89.4 us (22%)
  matrix products  32.8 us (8%)
  between operations  13.2 us (3%)
    all_gather x1, waiting for transfers between devices, per_device(): lax.all_gather(local_re, 'src', axis=1, tiled=True)  90.4 us
    all_gather x1, waiting for transfers between devices, per_device(): lax.all_gather(local_im, 'src', axis=1, tiled=True)  90.1 us
    all_to_all x1, blocking collectives, per_device(): lax.all_to_all(spectra, 'freq', split_axis=0, concat_axis=1, tiled=True)  89.4 us
    all_gather x1, waiting for transfers between devices, per_device(): piece_im = lax.all_gather(local_im, 'rcv', axis=2, tiled=True)  48.8 us
    all_gather x1, waiting for transfers between devices, per_device(): piece_re = lax.all_gather(local_re, 'rcv', axis=2, tiled=True)  39.8 us
    dot_general x4, matrix products, batched_dot(): jnp.einsum('mgq,mqn->mgn', left, right, precision=lax.Precision.HIGHEST,...  30.5 us
  transfers between devices with their start and end apart: 4, of which 4 were waited for; matrix products, arithmetic and copies ran while one was open for 4% of the time, Pallas kernels for 0%

commit v1 on v0

--- a/solution.py
+++ b/solution.py
@@ -54,7 +54,12 @@
         lax.all_gather(local_re, "src", axis=1, tiled=True),
         lax.all_gather(local_im, "src", axis=1, tiled=True),
     )
-    piece_re = lax.all_gather(local_re, "rcv", axis=2, tiled=True)
+    ring = [local_re]
+    for hop in range(7):
+        ring.append(lax.ppermute(ring[-1], "rcv", [(dev, (dev + 1) % 8) for dev in range(8)]))
+    piece_re = jnp.roll(
+        jnp.concatenate(ring[::-1], axis=2), (lax.axis_index("rcv") + 1) * ring[0].shape[2], axis=2
+    )
     piece_im = lax.all_gather(local_im, "rcv", axis=2, tiled=True)
     real_part, imag_part = complex_product(piece_re, piece_im, col_re, col_im)
     scale = -1.0 / math.sqrt(N)

time: 412 us -> 375 us (0.910)
  waiting for transfers between devices: 271 us -> 183 us
  local copies, waits for them, and re-layouts: 3.48 us -> 34.8 us
  starting transfers between devices: 0.3 us -> 18.4 us
    all_gather x1, waiting for transfers between devices: 90.1 us -> 0.01 us  [per_device(): lax.all_gather(local_im, 'src', axis=1, tiled=True)]
    ppermute x0 -> x7, waiting for transfers between devices: none -> 63.1 us  [per_device(): lax.ppermute(ring[-1], 'rcv', [(dev, (dev + 1) % 8) for dev in range(8)])]
    all_gather x1 -> x0, waiting for transfers between devices: 39.8 us -> none  [per_device(): piece_re = lax.all_gather(local_re, 'rcv', axis=2, tiled=True)]
    unnamed x9 -> x39, local copies, waits for them, and re-layouts: 2.13 us -> 31 us
    all_gather x1, waiting for transfers between devices: 48.8 us -> 29 us  [per_device(): piece_im = lax.all_gather(local_im, 'rcv', axis=2, tiled=True)]
    ppermute x0 -> x7, starting transfers between devices: none -> 18.3 us  [per_device(): lax.ppermute(ring[-1], 'rcv', [(dev, (dev + 1) % 8) for dev in range(8)])]
  transfers between devices with their start and end apart: 4 -> 10, of which waited for: 4 -> 9; matrix products, arithmetic and copies ran while one was open for 4% -> 9% of each run, Pallas kernels for 0% -> 0%
where the time goes in v1:
time: 375 us; the launch traced here: 374 us
  waiting for transfers between devices  183 us (49%)
  blocking collectives  89.4 us (24%)
  local copies, waits for them, and re-layouts  34.8 us (9%)
  matrix products  34 us (9%)
  starting transfers between devices  18.4 us (5%)
  between operations  13.3 us (4%)
    all_gather x1, waiting for transfers between devices, per_device(): lax.all_gather(local_re, 'src', axis=1, tiled=True)  90.1 us
    all_to_all x1, blocking collectives, per_device(): lax.all_to_all(spectra, 'freq', split_axis=0, concat_axis=1, tiled=True)  89.4 us
    ppermute x7, waiting for transfers between devices, per_device(): lax.ppermute(ring[-1], 'rcv', [(dev, (dev + 1) % 8) for dev in range(8)])  63.1 us
    dot_general x4, matrix products, batched_dot(): jnp.einsum('mgq,mqn->mgn', left, right, precision=lax.Precision.HIGHEST,...  31.7 us
    unnamed x39, local copies, waits for them, and re-layouts  31 us
    all_gather x1, waiting for transfers between devices, per_device(): piece_im = lax.all_gather(local_im, 'rcv', axis=2, tiled=True)  29 us
    ppermute x7, starting transfers between devices, per_device(): lax.ppermute(ring[-1], 'rcv', [(dev, (dev + 1) % 8) for dev in range(8)])  18.3 us
  transfers between devices with their start and end apart: 10, of which 9 were waited for; matrix products, arithmetic and copies ran while one was open for 9% of the time, Pallas kernels for 0%

profile of v1, /device:TPU:1, one launch (start us, length us, event | category | flops | bytes accessed | tf_op | source)
XLA Modules:
  0.0 374.3 jit_solution(9475179533054944335)
XLA Ops:
  8.1 2.3 fusion.41
  11.3 89.4 %all_to_all.15 = f32[192,16,128]{2,1,0:T(8,128)S(1)} all-to-all(f32[192,16,128]{2,1,0:T(8,128)S(1)} %copy.15), channel_id=1, replica_groups=mesh['freq'=32,'src'=2,'rcv'=8] {'freq'}, dimensions={0} | all-to-all | bytes 3145728 | tf_op jit(solution)/shard_map/all_to_all | solution.py:47
  104.3 3.4 collective-permute-start
  107.7 9.3 %collective-permute-done = f32[3,512,128]{2,1,0:T(8,128)S(1)} collective-permute-done((f32[3,512,128]{2,1,0:T(8,128)}, f32[3,512,128]{2,1,0:T(8,128)S(1)}, u32[]{:S(2)}, u32[]{:S(2)}) %collective-permute-start) | collective-permute-done | bytes 786464 | tf_op jit(solution)/shard_map/ppermute | solution.py:59
  117.0 2.4 collective-permute-start.1
  119.4 8.9 %collective-permute-done.1 = f32[3,512,128]{2,1,0:T(8,128)S(1)} collective-permute-done((f32[3,512,128]{2,1,0:T(8,128)S(1)}, f32[3,512,128]{2,1,0:T(8,128)S(1)}, u32[]{:S(2)}, u32[]{:S(2)}) %collective-permute-start.1) | collective-permute-done | bytes 786464 | tf_op jit(solution)/shard_map/ppermute | solution.py:59
  129.2 2.5 collective-permute-start.2
  131.7 8.9 %collective-permute-done.2 = f32[3,512,128]{2,1,0:T(8,128)S(1)} collective-permute-done((f32[3,512,128]{2,1,0:T(8,128)S(1)}, f32[3,512,128]{2,1,0:T(8,128)S(1)}, u32[]{:S(2)}, u32[]{:S(2)}) %collective-permute-start.2) | collective-permute-done | bytes 786464 | tf_op jit(solution)/shard_map/ppermute | solution.py:59
  141.6 2.5 collective-permute-start.3
  144.0 8.9 %collective-permute-done.3 = f32[3,512,128]{2,1,0:T(8,128)S(1)} collective-permute-done((f32[3,512,128]{2,1,0:T(8,128)S(1)}, f32[3,512,128]{2,1,0:T(8,128)S(1)}, u32[]{:S(2)}, u32[]{:S(2)}) %collective-permute-start.3) | collective-permute-done | bytes 786464 | tf_op jit(solution)/shard_map/ppermute | solution.py:59
  154.0 2.5 collective-permute-start.4
  156.4 8.9 %collective-permute-done.4 = f32[3,512,128]{2,1,0:T(8,128)S(1)} collective-permute-done((f32[3,512,128]{2,1,0:T(8,128)S(1)}, f32[3,512,128]{2,1,0:T(8,128)S(1)}, u32[]{:S(2)}, u32[]{:S(2)}) %collective-permute-start.4) | collective-permute-done | bytes 786464 | tf_op jit(solution)/shard_map/ppermute | solution.py:59
  166.3 2.5 collective-permute-start.5
  168.7 8.9 %collective-permute-done.5 = f32[3,512,128]{2,1,0:T(8,128)} collective-permute-done((f32[3,512,128]{2,1,0:T(8,128)S(1)}, f32[3,512,128]{2,1,0:T(8,128)}, u32[]{:S(2)}, u32[]{:S(2)}) %collective-permute-start.5) | collective-permute-done | bytes 786464 | tf_op jit(solution)/shard_map/ppermute | solution.py:59
  177.7 2.6 collective-permute-start.6
  180.3 9.2 %collective-permute-done.6 = f32[3,512,128]{2,1,0:T(8,128)} collective-permute-done((f32[3,512,128]{2,1,0:T(8,128)}, f32[3,512,128]{2,1,0:T(8,128)}, u32[]{:S(2)}, u32[]{:S(2)}) %collective-permute-start.6) | collective-permute-done | bytes 786464 | tf_op jit(solution)/shard_map/ppermute | solution.py:59
  205.4 2.2 constant_dynamic-update-slice_fusion.7
  207.6 2.2 constant_dynamic-update-slice_fusion.6
  215.8 29.0 %all-gather.9.cloned.1.call-done = f32[3,1,512,1024]{3,2,0,1:T(8,128)} async-done(((f32[3,1,512,128]{3,2,0,1:T(8,128)}), f32[3,1,512,1024]{3,2,0,1:T(8,128)}) %all-gather.9.cloned.1.call-update) | async-done | bytes 6291472 | tf_op jit(solution)/shard_map/all_gather | solution.py:63
  244.8 7.9 %fusion.2 = f32[3,512,128]{2,1,0:T(8,128)S(1)} fusion(f32[3,1,512,1024]{3,2,0,1:T(8,128)} %all-gather.9.cloned.1.call-done, f32[3,1,1024,128]{3,2,0,1:T(8,128)} %all-gather.11.cloned.1.call-done), kind=kOutput, calls=%fused_computation.2 | convolution fusion | flops 2415919104 | bytes 8650752 | tf_op jit(solution)/shard_map/mgq,mqn->mgn/dot_general | solution.py:21
  252.7 90.1 %all-gather.7.cloned.1.call-done = f32[3,1,1024,128]{3,2,0,1:T(8,128)} async-done(((f32[3,1,512,128]{3,2,0,1:T(8,128)}), f32[3,1,1024,128]{3,2,0,1:T(8,128)}) %all-gather.7.cloned.1.call-update) | async-done | bytes 1572880 | tf_op jit(solution)/shard_map/all_gather | solution.py:54
  342.8 8.1 %fusion = f32[3,512,128]{2,1,0:T(8,128)S(1)} fusion(f32[3,1,512,1024]{3,2,0,1:T(8,128)} %all-gather.9.cloned.1.call-done, f32[3,1,1024,128]{3,2,0,1:T(8,128)} %all-gather.7.cloned.1.call-done), kind=kOutput, calls=%fused_computation | convolution fusion | flops 2415919104 | bytes 8650752 | tf_op jit(solution)/shard_map/mgq,mqn->mgn/dot_general | solution.py:21
  350.9 8.0 %fusion.17 = f32[1,3,512,128]{3,2,1,0:T(8,128)S(1)} fusion(f32[3,512,128]{2,1,0:T(8,128)S(1)} %fusion.2, f32[3,1,1024,128]{3,2,0,1:T(8,128)} %all-gather.7.cloned.1.call-done, f32[3,512,2048]{2,1,0:T(8,128)} %constant_dynamic-update-slice_fusion, s32[]{:T(128)S(6)} %select_n.34), kind=kOutput, calls=%fused_computation.14 | convolution fusion | flops 2416115712 | bytes 9437188 | tf_op jit(solution)/shard_map/mgq,mqn->mgn/dot_general | solution.py:21
  358.9 7.7 %fusion.27 = f32[1,3,512,128]{3,2,1,0:T(8,128)S(1)} fusion(f32[3,512,128]{2,1,0:T(8,128)S(1)} %fusion, f32[3,1,1024,128]{3,2,0,1:T(8,128)S(1)} %copy-done.3, f32[3,512,2048]{2,1,0:T(8,128)} %constant_dynamic-update-slice_fusion, s32[]{:T(128)S(6)} %select_n.34), kind=kOutput, calls=%fused_computation.16 | convolution fusion | flops 2416115712 | bytes 9437188 | tf_op jit(solution)/shard_map/mgq,mqn->mgn/dot_general | solution.py:21
  (53 shorter events, 32.9 us)
Async XLA Ops:
  6.5 1.6 copy-start
  6.5 209.2 %all-gather.11.cloned.1.call-start = ((), (), s32[]{:S(2)}) async-start(), calls=%async_computation.3 | async-start | bytes 2359296 | tf_op jit(solution)/shard_map/all_gather | solution.py:55
  100.9 1.1 copy-start.1
  103.5 141.2 %all-gather.9.cloned.1.call-start = ((), (), s32[]{:S(2)}) async-start(), calls=%async_computation.2 | async-start | bytes 7077888 | tf_op jit(solution)/shard_map/all_gather | solution.py:63
  104.3 238.5 %all-gather.7.cloned.1.call-start = ((), (), s32[]{:S(2)}) async-start(), calls=%async_computation.1 | async-start | bytes 2359296 | tf_op jit(solution)/shard_map/all_gather | solution.py:54
  104.3 12.7 %collective-permute-start = (f32[3,512,128]{2,1,0:T(8,128)}, f32[3,512,128]{2,1,0:T(8,128)S(1)}, u32[]{:S(2)}, u32[]{:S(2)}) collective-permute-start(f32[3,512,128]{2,1,0:T(8,128)} %get-tuple-element.5), channel_id=1, source_target_pairs={{0,1},{1,2},{2,3},{3,4},{4,5},{5,6},{6,7},{7,0},{8,9},{9,10},{10,1... | collective-permute-start | bytes 2359304 | tf_op jit(solution)/shard_map/ppermute | solution.py:59
  117.0 11.3 %collective-permute-start.1 = (f32[3,512,128]{2,1,0:T(8,128)S(1)}, f32[3,512,128]{2,1,0:T(8,128)S(1)}, u32[]{:S(2)}, u32[]{:S(2)}) collective-permute-start(f32[3,512,128]{2,1,0:T(8,128)S(1)} %collective-permute-done), channel_id=1, source_target_pairs={{0,1},{1,2},{2,3},{3,4},{4,5},{5,6},{6,7},{7,0},{8,9},{9,10},{10,1... | collective-permute-start | bytes 2359304 | tf_op jit(solution)/shard_map/ppermute | solution.py:59
  128.3 0.9 copy-start.4
  129.2 11.4 %collective-permute-start.2 = (f32[3,512,128]{2,1,0:T(8,128)S(1)}, f32[3,512,128]{2,1,0:T(8,128)S(1)}, u32[]{:S(2)}, u32[]{:S(2)}) collective-permute-start(f32[3,512,128]{2,1,0:T(8,128)S(1)} %collective-permute-done.1), channel_id=1, source_target_pairs={{0,1},{1,2},{2,3},{3,4},{4,5},{5,6},{6,7},{7,0},{8,9},{9,10},{10,1... | collective-permute-start | bytes 2359304 | tf_op jit(solution)/shard_map/ppermute | solution.py:59
  140.6 1.0 copy-start.6
  141.6 11.4 %collective-permute-start.3 = (f32[3,512,128]{2,1,0:T(8,128)S(1)}, f32[3,512,128]{2,1,0:T(8,128)S(1)}, u32[]{:S(2)}, u32[]{:S(2)}) collective-permute-start(f32[3,512,128]{2,1,0:T(8,128)S(1)} %collective-permute-done.2), channel_id=1, source_target_pairs={{0,1},{1,2},{2,3},{3,4},{4,5},{5,6},{6,7},{7,0},{8,9},{9,10},{10,1... | collective-permute-start | bytes 2359304 | tf_op jit(solution)/shard_map/ppermute | solution.py:59
  153.0 1.0 copy-start.8
  154.0 11.4 %collective-permute-start.4 = (f32[3,512,128]{2,1,0:T(8,128)S(1)}, f32[3,512,128]{2,1,0:T(8,128)S(1)}, u32[]{:S(2)}, u32[]{:S(2)}) collective-permute-start(f32[3,512,128]{2,1,0:T(8,128)S(1)} %collective-permute-done.3), channel_id=1, source_target_pairs={{0,1},{1,2},{2,3},{3,4},{4,5},{5,6},{6,7},{7,0},{8,9},{9,10},{10,1... | collective-permute-start | bytes 2359304 | tf_op jit(solution)/shard_map/ppermute | solution.py:59
  165.4 0.9 copy-start.10
  166.3 11.4 %collective-permute-start.5 = (f32[3,512,128]{2,1,0:T(8,128)S(1)}, f32[3,512,128]{2,1,0:T(8,128)}, u32[]{:S(2)}, u32[]{:S(2)}) collective-permute-start(f32[3,512,128]{2,1,0:T(8,128)S(1)} %collective-permute-done.4), channel_id=1, source_target_pairs={{0,1},{1,2},{2,3},{3,4},{4,5},{5,6},{6,7},{7,0},{8,9},{9,10},{10,1... | collective-permute-start | bytes 2359304 | tf_op jit(solution)/shard_map/ppermute | solution.py:59
  177.7 11.8 %collective-permute-start.6 = (f32[3,512,128]{2,1,0:T(8,128)}, f32[3,512,128]{2,1,0:T(8,128)}, u32[]{:S(2)}, u32[]{:S(2)}) collective-permute-start(f32[3,512,128]{2,1,0:T(8,128)} %collective-permute-done.5), channel_id=1, source_target_pairs={{0,1},{1,2},{2,3},{3,4},{4,5},{5,6},{6,7},{7,0},{8,9},{9,10},{10,1... | collective-permute-start | bytes 2359304 | tf_op jit(solution)/shard_map/ppermute | solution.py:59
  180.3 29.5 %copy-start.11 = (f32[3,512,128]{2,1,0:T(8,128)S(1)}, f32[3,512,128]{2,1,0:T(8,128)}, u32[]{:S(2)}) copy-start(f32[3,512,128]{2,1,0:T(8,128)} %copy-done.10) | copy-start | bytes 2359300
  180.3 30.4 %copy-start.9 = (f32[3,512,128]{2,1,0:T(8,128)S(1)}, f32[3,512,128]{2,1,0:T(8,128)}, u32[]{:S(2)}) copy-start(f32[3,512,128]{2,1,0:T(8,128)} %copy-done.8) | copy-start | bytes 2359300
  180.3 31.5 %copy-start.7 = (f32[3,512,128]{2,1,0:T(8,128)S(1)}, f32[3,512,128]{2,1,0:T(8,128)}, u32[]{:S(2)}) copy-start(f32[3,512,128]{2,1,0:T(8,128)} %copy-done.6) | copy-start | bytes 2359300
  180.3 32.4 %copy-start.5 = (f32[3,512,128]{2,1,0:T(8,128)S(1)}, f32[3,512,128]{2,1,0:T(8,128)}, u32[]{:S(2)}) copy-start(f32[3,512,128]{2,1,0:T(8,128)} %copy-done.4) | copy-start | bytes 2359300
  180.3 34.4 %copy-start.2 = (f32[6,32,16,128]{3,2,1,0:T(8,128)S(1)}, f32[6,32,16,128]{3,2,1,0:T(8,128)}, u32[]{:S(2)}) copy-start(f32[6,32,16,128]{3,2,1,0:T(8,128)} %copy-done.1) | copy-start | bytes 4718596
  342.8 16.1 %copy-start.3 = (f32[3,1,1024,128]{3,2,0,1:T(8,128)S(1)}, f32[3,1,1024,128]{3,2,0,1:T(8,128)}, u32[]{:S(2)}) copy-start(f32[3,1,1024,128]{3,2,0,1:T(8,128)} %all-gather.11.cloned.1.call-done) | copy-start | bytes 4718596
Sparse Core Ops, SparseCore 0:
  103.6 92.2 all-gather.10
  198.0 46.6 all-gather.8
  246.9 95.8 all-gather.6
